TPU v7x, 256 devices: a whole 4x4x8 slice. The times are simulated.
256 devices in a mesh: mem: 16 (over z, x_lo), lon: 16 (over x_hi, y, core).
Axes of the slice: x: 4 (x_hi: 2, x_lo: 2; x = x_hi * 2 + x_lo), y: 4, z: 8, core: 2. Of those that a mesh axis runs over, the one named last changes fastest.
Arguments:
- state: bfloat16 [256, 65536], P('mem', 'lon'), may hold values from -6 to 6
- hx: bfloat16 [512, 256, 128], P('lon'), may hold values from -6 to 6
- obs_value: float32 [512, 128], P('lon'), may hold values from -10 to 10
- obs_rinv: float32 [512, 128], P('lon'), may hold values from 0.3 to 3
- obs_count: int32 [512], P('lon'), may hold values from 1 to 128
- loc_pattern: int32 [512, 8], P('lon'), may hold values from 0 to 95, as said below
Outputs:
- analysis: bfloat16 [256, 65536], P('mem', 'lon')
Inputs may be any that keep to these rules, and one draw needn't show every extreme that they name: obs_count[n] is how many of block n's first observations are valid; the rest are ignored. Each row of loc_pattern holds 8 different window positions out of 96: the previous region's blocks, the patch's own region's blocks, the next region's blocks, around the closed longitude loop.
All inputs are finite; a program needn't handle non-finite values.
Results may differ from a plain program's by a relative error of at most 0.0065.
Values may be sent and summed in bfloat16 or wider, within the bound.
A program may use at most 64 MiB of HBM per device.

v0:
```python
import jax
import jax.numpy as jnp
from jax import lax
from jax.sharding import PartitionSpec as P

PAT_DEV = 2
USE = 8
ITERS = 6


def extended(value, sides, width):
    for axis, dim in sides:
        count, length = (lax.axis_size(axis), value.shape[dim])
        up = [(i, (i + 1) % count) for i in range(count)]
        down = [(j, i) for i, j in up]
        last = lax.slice_in_dim(value, length - width, length, axis=dim)
        first = lax.slice_in_dim(value, 0, width, axis=dim)
        before = lax.ppermute(last, axis, up)
        after = lax.ppermute(first, axis, down)
        value = jnp.concatenate([before, value, after], axis=dim)
    return value


def body(state, hx, obs_value, obs_rinv, obs_count, loc_pattern):
    high = lax.Precision.HIGHEST
    blocks = hx.shape[0]
    members = hx.shape[1]
    width_obs = hx.shape[2]
    mem_total = lax.axis_size("mem")
    mem_here = lax.axis_index("mem")
    region_patches = mem_total * PAT_DEV
    obs_mean = jnp.sum(hx, axis=1, dtype=jnp.float32) / members
    obs_pert = (hx.astype(jnp.float32) - obs_mean[:, None, :]).astype(jnp.bfloat16)
    valid = lax.broadcasted_iota(jnp.int32, (blocks, width_obs), 1) < obs_count[:, None]
    weight = jnp.where(valid, obs_rinv, jnp.float32(0.0))
    stats = jnp.stack([weight, weight * (obs_value - obs_mean)], axis=1).astype(jnp.bfloat16)
    picks = lax.dynamic_slice_in_dim(loc_pattern, mem_here * PAT_DEV, PAT_DEV, 0)
    ranks = (mem_here * PAT_DEV + jnp.arange(PAT_DEV, dtype=jnp.int32)).astype(jnp.float32)
    offset = (
        (picks.astype(jnp.float32) + 0.5) / blocks - 1.0 - (ranks[:, None] + 0.5) / region_patches
    )
    taper = jnp.exp(-0.5 * offset * offset)
    eye = jnp.eye(members, dtype=jnp.float32)
    system = jnp.broadcast_to((members - 1.0) * eye, (PAT_DEV, members, members))
    forcing = jnp.zeros((PAT_DEV, members), jnp.float32)
    window_pert, window_stats = (
        extended(obs_pert, (("lon", 0),), blocks),
        extended(stats, (("lon", 0),), blocks),
    )
    for slot in range(USE):
        chosen = picks[:, slot]
        picked_pert = window_pert[chosen]
        picked_stats = window_stats[chosen]
        scaled = (
            picked_stats[:, 0, None, :].astype(jnp.float32) * picked_pert.astype(jnp.float32)
        ).astype(jnp.bfloat16)
        gram = jnp.einsum("pkb,plb->pkl", picked_pert, scaled, preferred_element_type=jnp.float32)
        vec = jnp.einsum(
            "pkb,pb->pk", picked_pert, picked_stats[:, 1], preferred_element_type=jnp.float32
        )
        system = system + taper[:, slot, None, None] * gram
        forcing = forcing + taper[:, slot, None] * vec
    scale = jnp.sqrt(jnp.sum(system * system, axis=(1, 2)))
    iterate = system / scale[:, None, None]
    root = jnp.broadcast_to(eye, (PAT_DEV, members, members))
    for step in range(ITERS):
        factor = 1.5 * eye - 0.5 * jnp.einsum("pij,pjk->pik", root, iterate, precision=high)
        iterate = jnp.einsum("pij,pjk->pik", iterate, factor, precision=high)
        root = jnp.einsum("pij,pjk->pik", factor, root, precision=high)
    root = root / jnp.sqrt(scale)[:, None, None]
    inner = jnp.einsum("pij,pj->pi", root, forcing, precision=high)
    mean_weight = jnp.einsum("pij,pj->pi", root, inner, precision=high)
    transform = jnp.sqrt(jnp.float32(members - 1.0)) * root + mean_weight[:, :, None]
    local_members = state.shape[0]
    grid = state.reshape(local_members, region_patches, -1)
    gathered = lax.all_to_all(grid, "mem", split_axis=1, concat_axis=0, tiled=True)
    state_mean = jnp.sum(gathered, axis=0, dtype=jnp.float32) / members
    deviation = gathered.astype(jnp.float32) - state_mean[None]
    updated = state_mean[None] + jnp.einsum("pkl,kpt->lpt", transform, deviation, precision=high)
    result = lax.all_to_all(
        updated.astype(jnp.bfloat16), "mem", split_axis=0, concat_axis=1, tiled=True
    )
    return result.reshape(local_members, -1)


def solution(mesh):
    in_specs = (
        P("mem", "lon"),
        P("lon", None, None),
        P("lon", None),
        P("lon", None),
        P("lon"),
        P("lon", None),
    )
    out_specs = P("mem", "lon")
    return jax.shard_map(body, mesh=mesh, in_specs=in_specs, out_specs=out_specs, check_vma=False)
```

profile of v0, /device:TPU:4, one launch (start us, length us, event | category | flops | bytes accessed | tf_op | source)
XLA Modules:
  0.0 112.8 jit_solution(15731651959545263145)
XLA Ops:
  0.0 2.0 %convert_reduce_fusion = f32[32,128]{1,0:T(8,128)S(1)} fusion(bf16[32,256,128]{2,1,0:T(8,128)(2,1)} %param.7), kind=kLoop, calls=%fused_computation.18 | loop fusion | flops 2093056 | bytes 2113536 | tf_op jit(solution)/shard_map/reduce_sum | solution.py:32
  2.0 0.8 fusion.38
  2.8 0.8 fusion.39
  3.8 5.3 %collective-permute-start.3 = (bf16[32,2,128]{2,1,0:T(2,128)(2,1)S(1)}, bf16[32,2,128]{2,1,0:T(2,128)(2,1)S(1)}, u32[]{:S(2)}, u32[]{:S(2)}) collective-permute-start(bf16[32,2,128]{2,1,0:T(2,128)(2,1)S(1)} %pad_maximum_fusion.2), channel_id=1, source_target_pairs={{1,0},{2,1},{3,2},{4,3},{5,4},{6,5},{7,6},{8,7},{9,8},{10,9},{11,1... | collective-permute-start | bytes 49160 | tf_op jit(solution)/shard_map/ppermute | solution.py:19
  9.1 2.2 %fusion = bf16[32,256,128]{2,1,0:T(8,128)(2,1)S(1)} fusion(bf16[32,256,128]{2,1,0:T(8,128)(2,1)} %param.7, f32[32,128]{1,0:T(8,128)S(1)} %get-tuple-element.8), kind=kLoop, calls=%fused_computation.19 | loop fusion | flops 3145728 | bytes 4210688 | tf_op jit(solution)/shard_map/convert_element_type | solution.py:33
  11.4 5.3 %collective-permute-start.1 = (bf16[32,256,128]{2,1,0:T(8,128)(2,1)S(1)}, bf16[32,256,128]{2,1,0:T(8,128)(2,1)}, u32[]{:S(2)}, u32[]{:S(2)}) collective-permute-start(bf16[32,256,128]{2,1,0:T(8,128)(2,1)S(1)} %fusion), channel_id=1, source_target_pairs={{1,0},{2,1},{3,2},{4,3},{5,4},{6,5},{7,6},{8,7},{9,8},{10,9},{11,1... | collective-permute-start | bytes 6291464 | tf_op jit(solution)/shard_map/ppermute | solution.py:19
  16.7 0.7 copy_bitcast_fusion
  17.4 9.2 %all-to-all-start = ((bf16[16,32,128]{2,0,1:T(8,128)(2,1)}), bf16[16,32,128]{2,0,1:T(8,128)(2,1)S(1)}, u32[]{:S(2)}, u32[]{:S(2)}) async-start(bf16[16,32,128]{2,0,1:T(8,128)(2,1)} %copy_bitcast_fusion), calls=%async_computation | async-start | bytes 262144 | tf_op jit(solution)/shard_map/all_to_all | solution.py:76
  27.0 0.6 gather_fusion.13
  27.6 0.6 gather_fusion.11
  28.2 0.6 gather_fusion.9
  28.7 0.6 gather_fusion.7
  29.3 0.6 gather_fusion.5
  29.9 0.6 gather_fusion.3
  30.4 0.6 gather_fusion.15
  31.1 0.6 gather_fusion.1
  31.7 11.7 %all-to-all-done = bf16[16,32,128]{2,0,1:T(8,128)(2,1)S(1)} async-done(((bf16[16,32,128]{2,0,1:T(8,128)(2,1)}), bf16[16,32,128]{2,0,1:T(8,128)(2,1)S(1)}, u32[]{:S(2)}, u32[]{:S(2)}) %all-to-all-start) | async-done | bytes 131104 | tf_op jit(solution)/shard_map/all_to_all | solution.py:76
  43.5 0.7 bitcast_subtract_fusion
  44.2 5.5 %pad_maximum_fusion = bf16[96,256,128]{2,1,0:T(8,128)(2,1)} fusion(bf16[32,256,128]{2,1,0:T(8,128)(2,1)} %collective-permute-done.1, bf16[32,256,128]{2,1,0:T(8,128)(2,1)S(1)} %fusion, bf16[32,256,128]{2,1,0:T(8,128)(2,1)} %collective-permute-done), kind=kLoop, calls=%fused_computation.16 | loop fusion | flops 6291456 | bytes 12582912 | tf_op jit(solution)/shard_map/concatenate | solution.py:20
  49.8 3.4 %gather_fusion.12 = bf16[2,256,128]{2,1,0:T(8,128)(2,1)S(1)} fusion(bf16[96,256,128]{2,1,0:T(8,128)(2,1)} %pad_maximum_fusion, s32[1024]{0:T(1024)S(1)} %get-tuple-element.30), kind=kCustom, calls=%fused_computation.12 | custom fusion | bytes 262152 | tf_op jit(solution)/shard_map/gather | solution.py:52
  53.1 3.4 %gather_fusion.10 = bf16[2,256,128]{2,1,0:T(8,128)(2,1)S(1)} fusion(bf16[96,256,128]{2,1,0:T(8,128)(2,1)} %pad_maximum_fusion, s32[1024]{0:T(1024)S(1)} %get-tuple-element.31), kind=kCustom, calls=%fused_computation.10 | custom fusion | bytes 262152 | tf_op jit(solution)/shard_map/gather | solution.py:52
  56.5 3.4 %gather_fusion.8 = bf16[2,256,128]{2,1,0:T(8,128)(2,1)S(1)} fusion(bf16[96,256,128]{2,1,0:T(8,128)(2,1)} %pad_maximum_fusion, s32[1024]{0:T(1024)S(1)} %get-tuple-element.32), kind=kCustom, calls=%fused_computation.8 | custom fusion | bytes 262152 | tf_op jit(solution)/shard_map/gather | solution.py:52
  59.8 3.4 %gather_fusion.6 = bf16[2,256,128]{2,1,0:T(8,128)(2,1)S(1)} fusion(bf16[96,256,128]{2,1,0:T(8,128)(2,1)} %pad_maximum_fusion, s32[1024]{0:T(1024)S(1)} %get-tuple-element.33), kind=kCustom, calls=%fused_computation.6 | custom fusion | bytes 262152 | tf_op jit(solution)/shard_map/gather | solution.py:52
  63.2 3.4 %gather_fusion.4 = bf16[2,256,128]{2,1,0:T(8,128)(2,1)S(1)} fusion(bf16[96,256,128]{2,1,0:T(8,128)(2,1)} %pad_maximum_fusion, s32[1024]{0:T(1024)S(1)} %get-tuple-element.34), kind=kCustom, calls=%fused_computation.4 | custom fusion | bytes 262152 | tf_op jit(solution)/shard_map/gather | solution.py:52
  66.6 3.4 %gather_fusion.2 = bf16[2,256,128]{2,1,0:T(8,128)(2,1)S(1)} fusion(bf16[96,256,128]{2,1,0:T(8,128)(2,1)} %pad_maximum_fusion, s32[1024]{0:T(1024)S(1)} %get-tuple-element.35), kind=kCustom, calls=%fused_computation.2 | custom fusion | bytes 262152 | tf_op jit(solution)/shard_map/gather | solution.py:52
  69.9 3.4 %gather_fusion = bf16[2,256,128]{2,1,0:T(8,128)(2,1)S(1)} fusion(bf16[96,256,128]{2,1,0:T(8,128)(2,1)} %pad_maximum_fusion, s32[1024]{0:T(1024)S(1)} %get-tuple-element.36), kind=kCustom, calls=%fused_computation | custom fusion | bytes 262152 | tf_op jit(solution)/shard_map/gather | solution.py:52
  73.3 3.4 %gather_fusion.14 = bf16[2,256,128]{2,1,0:T(8,128)(2,1)S(1)} fusion(bf16[96,256,128]{2,1,0:T(8,128)(2,1)} %pad_maximum_fusion, s32[1024]{0:T(1024)S(1)} %get-tuple-element.29), kind=kCustom, calls=%fused_computation.14 | custom fusion | bytes 262152 | tf_op jit(solution)/shard_map/gather | solution.py:52
  76.8 0.1 fusion.55
  76.9 0.1 fusion.56
  77.1 0.1 fusion.57
  77.2 0.1 fusion.58
  77.4 0.1 fusion.59
  77.5 0.1 fusion.60
  77.7 0.1 fusion.53
  77.8 0.2 convolution_multiply_fusion.10
  78.1 0.2 convolution_multiply_fusion.11
  78.3 0.2 convolution_multiply_fusion.12
  78.6 0.2 convolution_multiply_fusion.7
  78.8 0.2 convolution_multiply_fusion.8
  79.0 0.2 convolution_multiply_fusion.9
  79.3 0.2 convolution_multiply_fusion.6
  79.5 0.5 multiply_reduce_fusion
  80.0 0.7 fusion.6
  80.7 0.7 fusion.35
  81.4 0.6 fusion.21
  82.1 0.7 fusion.5
  82.7 0.7 fusion.71
  83.4 0.7 fusion.70
  84.0 0.7 fusion.4
  84.7 0.7 fusion.73
  85.4 0.7 fusion.72
  86.0 0.7 fusion.3
  86.7 0.7 fusion.75
  87.4 0.7 fusion.74
  88.0 0.7 fusion.2
  88.7 0.7 fusion.77
  89.3 0.7 fusion.76
  90.0 0.9 fusion.1
  90.9 0.7 convolution_divide_fusion
  91.6 0.5 fusion.51
  92.2 0.6 fusion.49
  92.8 0.7 fusion.16
  93.6 18.3 %all_to_all.24 = bf16[256,2,128]{2,1,0:T(2,128)(2,1)S(1)} all-to-all(bf16[256,2,128]{2,1,0:T(2,128)(2,1)S(1)} %copy.46), channel_id=1, replica_groups=mesh['mem'=16,'lon'=16] {'mem'}, dimensions={0} | all-to-all | bytes 262144 | tf_op jit(solution)/shard_map/all_to_all | solution.py:80
  112.0 0.7 reshape.53
  (48 shorter events, 1.2 us)
Async XLA Ops:
  0.0 16.7 %copy-start = (bf16[16,4096]{1,0:T(8,128)(2,1)S(1)}, bf16[16,4096]{1,0:T(8,128)(2,1)}, u32[]{:S(2)}) copy-start(bf16[16,4096]{1,0:T(8,128)(2,1)} %param.6) | copy-start | bytes 393220
  0.0 26.7 %copy-start.2 = (s32[32,8]{0,1:T(8,128)S(1)}, s32[32,8]{0,1:T(8,128)}, u32[]{:S(2)}) copy-start(s32[32,8]{0,1:T(8,128)} %param.11) | copy-start | bytes 3076
  3.7 23.2 %collective-permute-start.2 = (bf16[32,2,128]{2,1,0:T(2,128)(2,1)S(1)}, bf16[32,2,128]{2,1,0:T(2,128)(2,1)S(1)}, u32[]{:S(2)}, u32[]{:S(2)}) collective-permute-start(bf16[32,2,128]{2,1,0:T(2,128)(2,1)S(1)} %pad_maximum_fusion.2), channel_id=1, source_target_pairs={{0,1},{1,2},{2,3},{3,4},{4,5},{5,6},{6,7},{7,8},{8,9},{9,10},{10,1... | collective-permute-start | bytes 49160 | tf_op jit(solution)/shard_map/ppermute | solution.py:18
  3.8 23.2 %collective-permute-start.3 = (bf16[32,2,128]{2,1,0:T(2,128)(2,1)S(1)}, bf16[32,2,128]{2,1,0:T(2,128)(2,1)S(1)}, u32[]{:S(2)}, u32[]{:S(2)}) collective-permute-start(bf16[32,2,128]{2,1,0:T(2,128)(2,1)S(1)} %pad_maximum_fusion.2), channel_id=1, source_target_pairs={{1,0},{2,1},{3,2},{4,3},{5,4},{6,5},{7,6},{8,7},{9,8},{10,9},{11,1... | collective-permute-start | bytes 49160 | tf_op jit(solution)/shard_map/ppermute | solution.py:19
  11.3 32.9 %collective-permute-start = (bf16[32,256,128]{2,1,0:T(8,128)(2,1)S(1)}, bf16[32,256,128]{2,1,0:T(8,128)(2,1)}, u32[]{:S(2)}, u32[]{:S(2)}) collective-permute-start(bf16[32,256,128]{2,1,0:T(8,128)(2,1)S(1)} %fusion), channel_id=1, source_target_pairs={{0,1},{1,2},{2,3},{3,4},{4,5},{5,6},{6,7},{7,8},{8,9},{9,10},{10,1... | collective-permute-start | bytes 6291464 | tf_op jit(solution)/shard_map/ppermute | solution.py:18
  11.4 32.8 %collective-permute-start.1 = (bf16[32,256,128]{2,1,0:T(8,128)(2,1)S(1)}, bf16[32,256,128]{2,1,0:T(8,128)(2,1)}, u32[]{:S(2)}, u32[]{:S(2)}) collective-permute-start(bf16[32,256,128]{2,1,0:T(8,128)(2,1)S(1)} %fusion), channel_id=1, source_target_pairs={{1,0},{2,1},{3,2},{4,3},{5,4},{6,5},{7,6},{8,7},{9,8},{10,9},{11,1... | collective-permute-start | bytes 6291464 | tf_op jit(solution)/shard_map/ppermute | solution.py:19
  17.4 25.9 %all-to-all-start = ((bf16[16,32,128]{2,0,1:T(8,128)(2,1)}), bf16[16,32,128]{2,0,1:T(8,128)(2,1)S(1)}, u32[]{:S(2)}, u32[]{:S(2)}) async-start(bf16[16,32,128]{2,0,1:T(8,128)(2,1)} %copy_bitcast_fusion), calls=%async_computation | async-start | bytes 262144 | tf_op jit(solution)/shard_map/all_to_all | solution.py:76
  86.7 6.1 %copy-start.1 = (f32[256,2,128]{2,0,1:T(8,128)S(1)}, f32[256,2,128]{2,0,1:T(8,128)}, u32[]{:S(2)}) copy-start(f32[256,2,128]{2,0,1:T(8,128)} %bitcast_subtract_fusion) | copy-start | bytes 786436
where the time goes:
time: 114 us; the launch traced here: 113 us
  local copies, waits for them, and re-layouts  33.2 us (29%)
  starting transfers between devices  20.1 us (18%)
  blocking collectives  18.3 us (16%)
  matrix products  16.5 us (14%)
  other arithmetic  12.5 us (11%)
  waiting for transfers between devices  11.7 us (10%)
    gather x8, local copies, waits for them, and re-layouts, body(): picked_pert = window_pert[chosen]  26.9 us
    all_to_all x1, blocking collectives, body(): lax.all_to_all(updated.astype(jnp.bfloat16), 'mem', split_axis=0, concat_...  18.3 us
    all_to_all x1, waiting for transfers between devices, body(): lax.all_to_all(grid, 'mem', split_axis=1, concat_axis=0, tiled=True)  11.7 us
    ppermute x2, starting transfers between devices, extended(): after = lax.ppermute(first, axis, down)  10.7 us
    all_to_all x1, starting transfers between devices, body(): lax.all_to_all(grid, 'mem', split_axis=1, concat_axis=0, tiled=True)  9.2 us
    concatenate x2, other arithmetic, extended(): value = jnp.concatenate([before, value, after], axis=dim)  5.6 us
    gather x8, local copies, waits for them, and re-layouts, body(): picked_stats = window_stats[chosen]  4.57 us
    dot_general x6, matrix products, body(): jnp.einsum('pij,pjk->pik', root, iterate, precision=high)  4.22 us
  transfers between devices with their start and end apart: 5, of which 1 were waited for; matrix products, arithmetic and copies ran while one was open for 8% of the time, Pallas kernels for 0%

commit v1 on v0

--- a/solution.py
+++ b/solution.py
@@ -77,9 +77,10 @@
     state_mean = jnp.sum(gathered, axis=0, dtype=jnp.float32) / members
     deviation = gathered.astype(jnp.float32) - state_mean[None]
     updated = state_mean[None] + jnp.einsum("pkl,kpt->lpt", transform, deviation, precision=high)
-    result = lax.all_to_all(
-        updated.astype(jnp.bfloat16), "mem", split_axis=0, concat_axis=1, tiled=True
-    )
+    part = updated.astype(jnp.bfloat16)
+    pieces = jnp.split(part, lax.axis_size("mem"), axis=0)
+    received = lax.all_to_all(jnp.stack(pieces), "mem", 0, 0)
+    result = jnp.concatenate(received, axis=1)
     return result.reshape(local_members, -1)
 
 

time: 114 us -> 115 us (level)
  local copies, waits for them, and re-layouts: 33.2 us -> 34.9 us
    another operation x0 -> x19, local copies, waits for them, and re-layouts: none -> 2.48 us  [the longest x18 1.75 us: body(): received = lax.all_to_all(jnp.stack(pieces), 'mem', 0, 0)]
  transfers between devices with their start and end apart: 5 -> 5, of which waited for: 1 -> 1; matrix products, arithmetic and copies ran while one was open for 8% -> 7% of each run, Pallas kernels for 0% -> 0%
where the time goes in v1:
time: 115 us
  local copies, waits for them, and re-layouts  34.9 us (30%)
  starting transfers between devices  20.1 us (17%)
  blocking collectives  18.3 us (16%)
  matrix products  16.5 us (14%)
  other arithmetic  12.6 us (11%)
  waiting for transfers between devices  11.7 us (10%)
    gather x8, local copies, waits for them, and re-layouts, body(): picked_pert = window_pert[chosen]  26.9 us
    all_to_all x1, blocking collectives, body(): received = lax.all_to_all(jnp.stack(pieces), 'mem', 0, 0)  18.3 us
    all_to_all x1, waiting for transfers between devices, body(): lax.all_to_all(grid, 'mem', split_axis=1, concat_axis=0, tiled=True)  11.7 us
    ppermute x2, starting transfers between devices, extended(): after = lax.ppermute(first, axis, down)  10.7 us
    all_to_all x1, starting transfers between devices, body(): lax.all_to_all(grid, 'mem', split_axis=1, concat_axis=0, tiled=True)  9.2 us
    concatenate x2, other arithmetic, extended(): value = jnp.concatenate([before, value, after], axis=dim)  5.66 us
    gather x8, local copies, waits for them, and re-layouts, body(): picked_stats = window_stats[chosen]  4.57 us
    dot_general x6, matrix products, body(): jnp.einsum('pij,pjk->pik', root, iterate, precision=high)  4.22 us
  transfers between devices with their start and end apart: 5, of which 1 were waited for; matrix products, arithmetic and copies ran while one was open for 7% of the time, Pallas kernels for 0%

profile of v1, /device:TPU:4, one launch (start us, length us, event | category | flops | bytes accessed | tf_op | source)
XLA Modules:
  0.0 114.6 jit_solution(14868526098098698818)
XLA Ops:
  0.0 2.0 %convert_reduce_fusion = f32[32,128]{1,0:T(8,128)S(1)} fusion(bf16[32,256,128]{2,1,0:T(8,128)(2,1)} %param.7), kind=kLoop, calls=%fused_computation.18 | loop fusion | flops 2093056 | bytes 2113536 | tf_op jit(solution)/shard_map/reduce_sum | solution.py:32
  2.0 0.8 fusion.38
  2.8 0.8 fusion.39
  3.8 5.3 %collective-permute-start.3 = (bf16[32,2,128]{2,1,0:T(2,128)(2,1)S(1)}, bf16[32,2,128]{2,1,0:T(2,128)(2,1)S(1)}, u32[]{:S(2)}, u32[]{:S(2)}) collective-permute-start(bf16[32,2,128]{2,1,0:T(2,128)(2,1)S(1)} %pad_maximum_fusion.2), channel_id=1, source_target_pairs={{1,0},{2,1},{3,2},{4,3},{5,4},{6,5},{7,6},{8,7},{9,8},{10,9},{11,1... | collective-permute-start | bytes 49160 | tf_op jit(solution)/shard_map/ppermute | solution.py:19
  9.1 2.2 %fusion = bf16[32,256,128]{2,1,0:T(8,128)(2,1)S(1)} fusion(bf16[32,256,128]{2,1,0:T(8,128)(2,1)} %param.7, f32[32,128]{1,0:T(8,128)S(1)} %get-tuple-element.24), kind=kLoop, calls=%fused_computation.19 | loop fusion | flops 3145728 | bytes 4210688 | tf_op jit(solution)/shard_map/convert_element_type | solution.py:33
  11.4 5.3 %collective-permute-start.1 = (bf16[32,256,128]{2,1,0:T(8,128)(2,1)S(1)}, bf16[32,256,128]{2,1,0:T(8,128)(2,1)}, u32[]{:S(2)}, u32[]{:S(2)}) collective-permute-start(bf16[32,256,128]{2,1,0:T(8,128)(2,1)S(1)} %fusion), channel_id=1, source_target_pairs={{1,0},{2,1},{3,2},{4,3},{5,4},{6,5},{7,6},{8,7},{9,8},{10,9},{11,1... | collective-permute-start | bytes 6291464 | tf_op jit(solution)/shard_map/ppermute | solution.py:19
  16.7 0.7 copy_bitcast_fusion
  17.4 9.2 %all-to-all-start = ((bf16[16,32,128]{2,0,1:T(8,128)(2,1)}), bf16[16,32,128]{2,0,1:T(8,128)(2,1)S(1)}, u32[]{:S(2)}, u32[]{:S(2)}) async-start(bf16[16,32,128]{2,0,1:T(8,128)(2,1)} %copy_bitcast_fusion), calls=%async_computation | async-start | bytes 262144 | tf_op jit(solution)/shard_map/all_to_all | solution.py:76
  27.0 0.6 gather_fusion.13
  27.6 0.6 gather_fusion.11
  28.2 0.6 gather_fusion.9
  28.7 0.6 gather_fusion.7
  29.3 0.6 gather_fusion.5
  29.9 0.6 gather_fusion.3
  30.4 0.6 gather_fusion.15
  31.1 0.6 gather_fusion.1
  31.7 11.7 %all-to-all-done = bf16[16,32,128]{2,0,1:T(8,128)(2,1)S(1)} async-done(((bf16[16,32,128]{2,0,1:T(8,128)(2,1)}), bf16[16,32,128]{2,0,1:T(8,128)(2,1)S(1)}, u32[]{:S(2)}, u32[]{:S(2)}) %all-to-all-start) | async-done | bytes 131104 | tf_op jit(solution)/shard_map/all_to_all | solution.py:76
  43.5 0.7 bitcast_subtract_fusion
  44.2 5.6 %pad_maximum_fusion = bf16[96,256,128]{2,1,0:T(8,128)(2,1)} fusion(bf16[32,256,128]{2,1,0:T(8,128)(2,1)} %collective-permute-done.1, bf16[32,256,128]{2,1,0:T(8,128)(2,1)S(1)} %fusion, bf16[32,256,128]{2,1,0:T(8,128)(2,1)} %collective-permute-done), kind=kLoop, calls=%fused_computation.16 | loop fusion | flops 6291456 | bytes 12582912 | tf_op jit(solution)/shard_map/concatenate | solution.py:20
  49.8 3.4 %gather_fusion.12 = bf16[2,256,128]{2,1,0:T(8,128)(2,1)S(1)} fusion(bf16[96,256,128]{2,1,0:T(8,128)(2,1)} %pad_maximum_fusion, s32[1024]{0:T(1024)S(1)} %get-tuple-element.46), kind=kCustom, calls=%fused_computation.12 | custom fusion | bytes 262152 | tf_op jit(solution)/shard_map/gather | solution.py:52
  53.2 3.4 %gather_fusion.10 = bf16[2,256,128]{2,1,0:T(8,128)(2,1)S(1)} fusion(bf16[96,256,128]{2,1,0:T(8,128)(2,1)} %pad_maximum_fusion, s32[1024]{0:T(1024)S(1)} %get-tuple-element.47), kind=kCustom, calls=%fused_computation.10 | custom fusion | bytes 262152 | tf_op jit(solution)/shard_map/gather | solution.py:52
  56.5 3.4 %gather_fusion.8 = bf16[2,256,128]{2,1,0:T(8,128)(2,1)S(1)} fusion(bf16[96,256,128]{2,1,0:T(8,128)(2,1)} %pad_maximum_fusion, s32[1024]{0:T(1024)S(1)} %get-tuple-element.48), kind=kCustom, calls=%fused_computation.8 | custom fusion | bytes 262152 | tf_op jit(solution)/shard_map/gather | solution.py:52
  59.9 3.4 %gather_fusion.6 = bf16[2,256,128]{2,1,0:T(8,128)(2,1)S(1)} fusion(bf16[96,256,128]{2,1,0:T(8,128)(2,1)} %pad_maximum_fusion, s32[1024]{0:T(1024)S(1)} %get-tuple-element.49), kind=kCustom, calls=%fused_computation.6 | custom fusion | bytes 262152 | tf_op jit(solution)/shard_map/gather | solution.py:52
  63.3 3.4 %gather_fusion.4 = bf16[2,256,128]{2,1,0:T(8,128)(2,1)S(1)} fusion(bf16[96,256,128]{2,1,0:T(8,128)(2,1)} %pad_maximum_fusion, s32[1024]{0:T(1024)S(1)} %get-tuple-element.50), kind=kCustom, calls=%fused_computation.4 | custom fusion | bytes 262152 | tf_op jit(solution)/shard_map/gather | solution.py:52
  66.6 3.4 %gather_fusion.2 = bf16[2,256,128]{2,1,0:T(8,128)(2,1)S(1)} fusion(bf16[96,256,128]{2,1,0:T(8,128)(2,1)} %pad_maximum_fusion, s32[1024]{0:T(1024)S(1)} %get-tuple-element.51), kind=kCustom, calls=%fused_computation.2 | custom fusion | bytes 262152 | tf_op jit(solution)/shard_map/gather | solution.py:52
  70.0 3.4 %gather_fusion = bf16[2,256,128]{2,1,0:T(8,128)(2,1)S(1)} fusion(bf16[96,256,128]{2,1,0:T(8,128)(2,1)} %pad_maximum_fusion, s32[1024]{0:T(1024)S(1)} %get-tuple-element.52), kind=kCustom, calls=%fused_computation | custom fusion | bytes 262152 | tf_op jit(solution)/shard_map/gather | solution.py:52
  73.4 3.4 %gather_fusion.14 = bf16[2,256,128]{2,1,0:T(8,128)(2,1)S(1)} fusion(bf16[96,256,128]{2,1,0:T(8,128)(2,1)} %pad_maximum_fusion, s32[1024]{0:T(1024)S(1)} %get-tuple-element.45), kind=kCustom, calls=%fused_computation.14 | custom fusion | bytes 262152 | tf_op jit(solution)/shard_map/gather | solution.py:52
  77.0 0.1 fusion.56
  77.2 0.1 fusion.57
  77.3 0.1 fusion.58
  77.5 0.1 fusion.59
  77.6 0.1 fusion.60
  77.8 0.1 fusion.53
  77.9 0.2 convolution_multiply_fusion.10
  78.2 0.2 convolution_multiply_fusion.11
  78.4 0.2 convolution_multiply_fusion.12
  78.6 0.2 convolution_multiply_fusion.7
  78.9 0.2 convolution_multiply_fusion.8
  79.1 0.2 convolution_multiply_fusion.9
  79.4 0.2 convolution_multiply_fusion.6
  79.6 0.5 multiply_reduce_fusion
  80.1 0.7 fusion.6
  80.8 0.7 fusion.35
  81.5 0.6 fusion.21
  82.1 0.7 fusion.5
  82.8 0.7 fusion.71
  83.4 0.7 fusion.70
  84.1 0.7 fusion.4
  84.8 0.7 fusion.73
  85.4 0.7 fusion.72
  86.1 0.7 fusion.3
  86.8 0.7 fusion.75
  87.4 0.7 fusion.74
  88.1 0.7 fusion.2
  88.7 0.7 fusion.77
  89.4 0.7 fusion.76
  90.1 0.9 fusion.1
  91.0 0.7 convolution_divide_fusion
  91.7 0.5 fusion.51
  92.2 0.6 fusion.49
  92.8 0.7 fusion.16
  93.6 0.3 slice_bitcast_fusion
  95.5 18.3 %all_to_all.14 = bf16[16,16,2,128]{3,1,2,0:T(8,128)(2,1)S(1)} all-to-all(bf16[16,16,2,128]{3,1,2,0:T(8,128)(2,1)S(1)} %constant_dynamic-update-slice_fusion), channel_id=1, replica_groups=mesh['mem'=16,'lon'=16] {'mem'}, dimensions={0} | all-to-all | bytes 262144 | tf_op jit(solution)/shard_map/all_to_all | solution.py:82
  113.9 0.7 reshape_reshape.3
  (79 shorter events, 2.7 us)
Async XLA Ops:
  0.0 16.7 %copy-start = (bf16[16,4096]{1,0:T(8,128)(2,1)S(1)}, bf16[16,4096]{1,0:T(8,128)(2,1)}, u32[]{:S(2)}) copy-start(bf16[16,4096]{1,0:T(8,128)(2,1)} %param.6) | copy-start | bytes 393220
  0.0 26.7 %copy-start.2 = (s32[32,8]{0,1:T(8,128)S(1)}, s32[32,8]{0,1:T(8,128)}, u32[]{:S(2)}) copy-start(s32[32,8]{0,1:T(8,128)} %param.11) | copy-start | bytes 3076
  3.7 23.2 %collective-permute-start.2 = (bf16[32,2,128]{2,1,0:T(2,128)(2,1)S(1)}, bf16[32,2,128]{2,1,0:T(2,128)(2,1)S(1)}, u32[]{:S(2)}, u32[]{:S(2)}) collective-permute-start(bf16[32,2,128]{2,1,0:T(2,128)(2,1)S(1)} %pad_maximum_fusion.2), channel_id=1, source_target_pairs={{0,1},{1,2},{2,3},{3,4},{4,5},{5,6},{6,7},{7,8},{8,9},{9,10},{10,1... | collective-permute-start | bytes 49160 | tf_op jit(solution)/shard_map/ppermute | solution.py:18
  3.8 23.2 %collective-permute-start.3 = (bf16[32,2,128]{2,1,0:T(2,128)(2,1)S(1)}, bf16[32,2,128]{2,1,0:T(2,128)(2,1)S(1)}, u32[]{:S(2)}, u32[]{:S(2)}) collective-permute-start(bf16[32,2,128]{2,1,0:T(2,128)(2,1)S(1)} %pad_maximum_fusion.2), channel_id=1, source_target_pairs={{1,0},{2,1},{3,2},{4,3},{5,4},{6,5},{7,6},{8,7},{9,8},{10,9},{11,1... | collective-permute-start | bytes 49160 | tf_op jit(solution)/shard_map/ppermute | solution.py:19
  11.3 32.9 %collective-permute-start = (bf16[32,256,128]{2,1,0:T(8,128)(2,1)S(1)}, bf16[32,256,128]{2,1,0:T(8,128)(2,1)}, u32[]{:S(2)}, u32[]{:S(2)}) collective-permute-start(bf16[32,256,128]{2,1,0:T(8,128)(2,1)S(1)} %fusion), channel_id=1, source_target_pairs={{0,1},{1,2},{2,3},{3,4},{4,5},{5,6},{6,7},{7,8},{8,9},{9,10},{10,1... | collective-permute-start | bytes 6291464 | tf_op jit(solution)/shard_map/ppermute | solution.py:18
  11.4 32.8 %collective-permute-start.1 = (bf16[32,256,128]{2,1,0:T(8,128)(2,1)S(1)}, bf16[32,256,128]{2,1,0:T(8,128)(2,1)}, u32[]{:S(2)}, u32[]{:S(2)}) collective-permute-start(bf16[32,256,128]{2,1,0:T(8,128)(2,1)S(1)} %fusion), channel_id=1, source_target_pairs={{1,0},{2,1},{3,2},{4,3},{5,4},{6,5},{7,6},{8,7},{9,8},{10,9},{11,1... | collective-permute-start | bytes 6291464 | tf_op jit(solution)/shard_map/ppermute | solution.py:19
  17.4 25.9 %all-to-all-start = ((bf16[16,32,128]{2,0,1:T(8,128)(2,1)}), bf16[16,32,128]{2,0,1:T(8,128)(2,1)S(1)}, u32[]{:S(2)}, u32[]{:S(2)}) async-start(bf16[16,32,128]{2,0,1:T(8,128)(2,1)} %copy_bitcast_fusion), calls=%async_computation | async-start | bytes 262144 | tf_op jit(solution)/shard_map/all_to_all | solution.py:76
  86.8 6.1 %copy-start.1 = (f32[256,2,128]{2,0,1:T(8,128)S(1)}, f32[256,2,128]{2,0,1:T(8,128)}, u32[]{:S(2)}) copy-start(f32[256,2,128]{2,0,1:T(8,128)} %bitcast_subtract_fusion) | copy-start | bytes 786436
